TPU v7x, 32 devices: a whole 2x2x4 slice. The times are simulated.
32 devices in a mesh: ctx: 8 (over y, x, core), head: 4 (over z).
Axes of the slice: x: 2, y: 2, z: 4, core: 2. Of those that a mesh axis runs over, the one named last changes fastest.
Arguments:
- input_queries: bfloat16 [8192, 6144], P(('ctx', 'head')), may hold values from -6 to 6
- input_keys: bfloat16 [8192, 1024], P(('ctx', 'head')), may hold values from -6 to 6
- input_values: bfloat16 [8192, 1024], P(('ctx', 'head')), may hold values from -6 to 6
- cotangent: bfloat16 [8192, 6144], P(('ctx', 'head')), may hold values from -6 to 6
- block_list: int32 [16, 8], replicated, may hold values from 0 to 15, as said below
- block_count: int32 [16], replicated, may hold values from 1 to 8, as said below
Outputs:
- attn_out: bfloat16 [8192, 6144], P(('ctx', 'head'))
- grad_query: bfloat16 [8192, 6144], P(('ctx', 'head'))
- key_gradient: bfloat16 [8192, 1024], P(('ctx', 'head'))
- value_gradient: bfloat16 [8192, 1024], P(('ctx', 'head'))
Inputs may be any that keep to these rules, and one draw needn't show every extreme that they name: `block_list`: row b lists entry 0 = b itself, then distinct blocks of other ctx indices up to position block_count[b] - 1, block c belonging to ctx index c // 2; entries from position block_count[b] on repeat b and are unused. The rows of the 2 query blocks of one ctx index together name at most one block of any other ctx index. `block_count`: query block 0 lists 8 blocks.
All inputs are finite; a program needn't handle non-finite values.
Results may differ from a plain program's by a relative error of at most 0.015.
Values may be sent and summed in bfloat16 or wider, within the bound.
No kernel may reach another device: no remote copies, remote signals or barrier semaphores. Data moves between devices by JAX's collectives and lax.ppermute only.
A program may use at most 128 MiB of HBM per device.

v0:
```python
import functools
import math

import jax
import jax.numpy as jnp
from jax import lax
from jax.experimental import pallas as pl
from jax.experimental.pallas import tpu as pltpu
from jax.sharding import PartitionSpec as P


QUERY_HEADS = 48
KEY_VALUE_HEADS = 8
HEAD_WIDTH = 128
BLOCK_TOKENS = 512
GROUP_WIDTH = QUERY_HEADS // KEY_VALUE_HEADS

SCORE_SCALE = HEAD_WIDTH ** (-0.5)
EXP2_SCALE = SCORE_SCALE * math.log2(math.e)
LOWEST = -3.0e38
VMEM_BYTES = 62 * 1024 * 1024


NT = (((1,), (1,)), ((), ()))
NN = (((1,), (0,)), ((), ()))
TN = (((0,), (0,)), ((), ()))


def dot(a, b, dims):
    return lax.dot_general(a, b, dims, preferred_element_type=jnp.float32)


def bf16(*shape):
    return jax.ShapeDtypeStruct(shape, jnp.bfloat16)


ANY = pl.BlockSpec(memory_space=pl.ANY)
VMEM = pl.BlockSpec(memory_space=pltpu.VMEM)
SMEM = pl.BlockSpec(memory_space=pltpu.SMEM)


class Copies:
    def __init__(self, sems):
        self.sems, self.made = sems, 0

    def make(self, src, dst):
        self.made += 1
        return pltpu.make_async_copy(src, dst, self.sems.at[self.made - 1])

    @staticmethod
    def run(copies):
        for copy in copies:
            copy.start()
        for copy in copies:
            copy.wait()


class Layout:
    def __init__(self, ctx_size, head_size, tokens):
        self.group = KEY_VALUE_HEADS
        assert ctx_size % self.group == 0
        self.ctx_size, self.heads, self.tokens = ctx_size, head_size, tokens
        self.line = ctx_size // self.group * head_size
        self.per_ctx = tokens * head_size // BLOCK_TOKENS
        self.per_block = BLOCK_TOKENS // tokens
        self.blocks = ctx_size * self.per_ctx
        self.others = range(1, self.group)

    def device(self, w, u):
        m, h = divmod(w, self.heads)
        return (m * self.group + u) * self.heads + h

    def swap(self, value, x):
        pairs = [
            (self.device(w, u), self.device(w, u ^ x))
            for w in range(self.line)
            for u in range(self.group)
        ]
        return lax.ppermute(value, ("ctx", "head"), pairs)

    def shift(self, value, sources, step):
        pairs = [
            (self.device(w, u), self.device(w + step, u)) for w in sources for u in range(self.group)
        ]
        return lax.ppermute(value, ("ctx", "head"), pairs)

    def place(self, w):
        m, h = w // self.heads, w % self.heads
        first = (m * self.per_ctx + h // self.per_block) * self.group
        return first, pl.multiple_of(h % self.per_block * self.tokens, self.tokens)

    def query_block(self, w, u):
        ctx = w // self.heads * self.group + u
        return ctx * self.per_ctx + w % self.heads // self.per_block

    def table_block(self, block, u):
        ctx = block // self.per_ctx
        first = (ctx // self.group * self.per_ctx + block % self.per_ctx) * self.group
        return first + jnp.bitwise_xor(ctx % self.group, u)


def copy_call(body, ins, specs, outs, n, out_spec=ANY):
    def kernel(*refs):
        sems = refs[-1]
        Copies.run(list(body(Copies(sems), refs[: len(ins)], refs[len(ins) : -1])))

    moved = 4 * sum(math.prod(o.shape) for o in outs)
    return pl.pallas_call(
        kernel,
        out_shape=outs,
        in_specs=specs,
        out_specs=[out_spec] * len(outs),
        scratch_shapes=[pltpu.SemaphoreType.DMA((n,))],
        compiler_params=pltpu.CompilerParams(vmem_limit_bytes=VMEM_BYTES),
        cost_estimate=pl.CostEstimate(flops=0, transcendentals=0, bytes_accessed=moved),
    )(*ins)


def columns(index, count=1):
    return pl.ds(pl.multiple_of(index * HEAD_WIDTH, HEAD_WIDTH), count * HEAD_WIDTH)


def pack(lay, u, arrays, count, places):
    def body(copies, ins, outs):
        rank, *raw = ins
        for x, out in zip(places, outs, strict=True):
            cols = columns(jnp.bitwise_xor(rank[0], x) * count, count)
            for half in range(2):
                yield copies.make(raw[half].at[:, cols], out.at[half])

    outs = [bf16(2, lay.tokens, count * HEAD_WIDTH)] * len(places)
    return copy_call(body, [u, *arrays], [SMEM, VMEM, VMEM], outs, 2 * len(places))


def pack_one(lay, u, array, count):
    def body(copies, ins, outs):
        rank, raw = ins
        for x, out in zip(lay.others, outs, strict=True):
            cols = columns(jnp.bitwise_xor(rank[0], x) * count, count)
            yield copies.make(raw.at[:, cols], out)

    outs = [bf16(lay.tokens, count * HEAD_WIDTH)] * len(lay.others)
    return copy_call(body, [u, array], [SMEM, VMEM], outs, len(outs))


def unpack(lay, u, slabs, count):
    flat, plan = [], []
    for out, some in enumerate(slabs):
        for x, part in enumerate(some):
            plan.append((out, x, len(flat)))
            flat.append(part)
    pairs = flat[0].ndim == 3

    def body(copies, ins, outs):
        rank, *parts = ins
        for out, x, at in plan:
            cols = columns(jnp.bitwise_xor(rank[0], x) * count, count)
            if pairs:
                for half in range(2):
                    yield copies.make(parts[at].at[half], outs[half].at[:, cols])
            else:
                yield copies.make(parts[at], outs[out].at[:, cols])

    outs = [bf16(lay.tokens, lay.group * count * HEAD_WIDTH)] * (2 if pairs else len(slabs))
    specs = [SMEM] + [ANY] * len(flat)
    return copy_call(body, [u, *flat], specs, outs, 2 * len(flat), VMEM)


def collect(lay, slabs):
    def body(copies, ins, outs):
        for x, part in enumerate(ins):
            for half in range(2):
                yield copies.make(part.at[half], outs[0].at[half, x])

    outs = [bf16(2, lay.group, lay.tokens, HEAD_WIDTH)]
    specs = [ANY] * lay.group
    return copy_call(body, list(slabs), specs, outs, 2 * lay.group, VMEM)[0]


def split(lay, terms):
    def kernel(*refs):
        ins, outs = refs[: len(terms)], refs[len(terms) :]
        for x, out in enumerate(outs):
            for half in range(2):
                total = ins[0][half, x].astype(jnp.float32)
                for term in ins[1:]:
                    total += term[half, x].astype(jnp.float32)
                out[half] = total.astype(jnp.bfloat16)

    outs = [bf16(2, lay.tokens, HEAD_WIDTH)] * lay.group
    moved = 2 * (len(terms) + 1) * math.prod(terms[0].shape)
    return pl.pallas_call(
        kernel,
        out_shape=outs,
        in_specs=[VMEM] * len(terms),
        out_specs=[VMEM] * len(outs),
        cost_estimate=pl.CostEstimate(flops=0, transcendentals=0, bytes_accessed=moved),
        name="split",
    )(*terms)


def wait_all(copies):
    for copy in copies:
        copy.wait()


def start_all(copies):
    for copy in copies:
        copy.start()


def start_guarded(guarded, run=start_all):
    for valid, some in guarded:

        @pl.when(valid)
        def _():
            run(some)


def at_place(x, lists, run):
    for place, some in lists.items():

        @pl.when(x == place)
        def _():
            run(some)


REPEAT = BLOCK_TOKENS // HEAD_WIDTH
COLS = [pl.ds(g * HEAD_WIDTH, HEAD_WIDTH) for g in range(GROUP_WIDTH)]


def widen(x):
    return jnp.concatenate([x] * REPEAT, axis=1)


def score_weights(s, top):
    return jnp.exp2((s - widen(top)) * EXP2_SCALE).astype(jnp.bfloat16)


def score_grads(e, cot, v, delta):
    return e * (dot(cot, v, NT) - widen(delta)).astype(jnp.bfloat16)


def table_copies(lay, made, plane, refs, table, into, base=0):
    first, row = lay.place(plane)
    part = pl.ds(first - base, lay.group), pl.ds(row, lay.tokens)
    if into:
        return [made.make(table.at[n], ref.at[part]) for n, ref in enumerate(refs)]
    return [made.make(ref.at[part], table.at[n]) for n, ref in enumerate(refs)]


def offsets(lay, w, below, above):
    for k in range(1, len(below) + 1):
        yield w >= k, w - k, below[k - 1]
        yield w + k < lay.line, w + k, above[k - 1]


def near_tables(lay, made, w, refs, own_table, below, above):
    first = lay.place(w)[0]
    guarded = []
    for valid, plane, table in offsets(lay, w, below, above):
        valid = valid & (lay.place(plane)[0] == first)
        guarded.append((valid, table_copies(lay, made, plane, refs, table, True, first)))
    return table_copies(lay, made, w, refs, own_table, True, first), guarded


def lane_max(m, s):
    for part in range(REPEAT):
        m = jnp.maximum(m, s[:, part * HEAD_WIDTH : (part + 1) * HEAD_WIDTH])
    return m


def values_and_ones(v):
    return jnp.concatenate([v, jnp.ones((BLOCK_TOKENS, HEAD_WIDTH), jnp.bfloat16)], axis=1)


def spread(column, shape):
    return jnp.broadcast_to(column, shape)


def near_forward_kernel(lay, list_ref, count_ref, where_ref, *refs):
    refs = list(refs)

    def take(n):
        taken = refs[:n]
        del refs[:n]
        return taken

    near = lay.per_block - 1
    raw, slabs = take(1)[0], take(lay.group - 1)
    own_table, below, above = take(1)[0], take(near), take(near)
    o_out, stat_out = take(2)
    q_scr, k_tab, v_tab, s_scr, m_scr, o_acc, o_scr, st_scr, sems = refs
    u, w = where_ref[0], where_ref[1]
    heads = GROUP_WIDTH
    made = Copies(sems)
    first = lay.place(w)[0]
    copies, guarded = near_tables(lay, made, w, (k_tab, v_tab), own_table, below, above)
    loads = {}
    for x in range(lay.group):
        src = slabs[x - 1] if x else raw.at[:, columns(u * heads, heads)]
        loads[x] = [made.make(src, q_scr.at[x])]
    start_all(copies)
    start_guarded(guarded)
    for some in loads.values():
        start_all(some)
    wait_all(copies)
    start_guarded(guarded, wait_all)
    shape = (lay.tokens, HEAD_WIDTH)
    lane = lax.broadcasted_iota(jnp.int32, shape, 1)
    saves = {
        x: [made.make(o_scr.at[x % 2], o_out.at[x]), made.make(st_scr.at[x], stat_out.at[x])]
        for x in range(lay.group)
    }

    def one(x, carry):
        at_place(x, loads, wait_all)
        at_place(x, {p + 2: some for p, some in saves.items()}, lambda c: wait_all(c[:1]))
        mine = lay.query_block(w, jnp.bitwise_xor(u, x))
        live = count_ref[mine]
        m_scr[...] = jnp.full_like(m_scr, LOWEST)

        def scores(i, c):
            block = lay.table_block(list_ref[mine, i], u) - first

            @pl.when((block >= 0) & (block < lay.group))
            def _():
                for g in range(heads):
                    s = dot(q_scr[x, :, COLS[g]], k_tab[block], NT)
                    s_scr[i, g] = s
                    m_scr[g] = lane_max(m_scr[g], s)

            return c

        lax.fori_loop(0, live, scores, 0)
        stats = jnp.zeros(shape, jnp.float32)
        for g in range(heads):
            top = spread(jnp.max(m_scr[g], axis=1, keepdims=True), shape)
            m_scr[g] = top
            stats = jnp.where(lane == g, top, stats)
        o_acc[...] = jnp.zeros_like(o_acc)

        def weigh(i, c):
            block = lay.table_block(list_ref[mine, i], u) - first

            @pl.when((block >= 0) & (block < lay.group))
            def _():
                v_ones = values_and_ones(v_tab[block])
                for g in range(heads):
                    o_acc[g] += dot(score_weights(s_scr[i, g], m_scr[g]), v_ones, NN)

            return c

        lax.fori_loop(0, live, weigh, 0)
        for g in range(heads):
            o_scr[x % 2, :, COLS[g]] = o_acc[g, :, :HEAD_WIDTH]
            stats = jnp.where(lane == heads + g, o_acc[g, :, HEAD_WIDTH:], stats)
        st_scr[x] = stats
        at_place(x, saves, start_all)
        return carry

    lax.fori_loop(0, lay.group, one, 0)
    for x, some in saves.items():
        wait_all(some if x >= lay.group - 2 else some[1:])


def forward_kernel(lay, list_ref, count_ref, where_ref, *refs):
    refs = list(refs)

    def take(n):
        taken = refs[:n]
        del refs[:n]
        return taken

    raw, q_slabs, do_slabs = take(2), take(lay.group - 1), take(lay.group - 1)
    o_in, stat_in = take(2)
    below, above = take(lay.line - 1), take(lay.line - 1)
    outs, (do_out, stat_out, gq_out) = take(lay.group), take(3)
    to_below, to_above = take(lay.line - 1), take(lay.line - 1)
    q_scr, do_scr, sum_scr, k_tab, v_tab, dk_acc, dv_acc, s_scr, e_scr, m_scr = refs[:10]
    o_acc, o_scr, st_scr, sems = refs[10:]
    u, w = where_ref[0], where_ref[1]
    heads = GROUP_WIDTH
    made = Copies(sems)
    first = lay.place(w)[0]

    def far_base(plane):
        return jnp.where(lay.place(plane)[0] > first, lay.group, 0)

    def far_copies(below, above, into):
        return [
            (
                valid & (lay.place(plane)[0] != first),
                table_copies(lay, made, plane, (k_tab, v_tab), table, into, far_base(plane)),
            )
            for valid, plane, table in offsets(lay, w, below, above)
        ]

    guarded = far_copies(below, above, True)
    loads = {}
    for x in range(lay.group):
        cols = columns(u * heads, heads)
        loads[x] = [
            made.make(q_slabs[x - 1] if x else raw[0].at[:, cols], q_scr.at[x]),
            made.make(do_slabs[x - 1] if x else raw[1].at[:, cols], do_scr.at[x]),
            made.make(o_in.at[x], sum_scr.at[x]),
            made.make(stat_in.at[x], st_scr.at[x]),
        ]
    start_guarded(guarded)
    for some in loads.values():
        start_all(some)
    dk_acc[...] = jnp.zeros_like(dk_acc)
    dv_acc[...] = jnp.zeros_like(dv_acc)
    start_guarded(guarded, wait_all)

    shape = (lay.tokens, HEAD_WIDTH)
    lane = lax.broadcasted_iota(jnp.int32, shape, 1)
    saves = {
        x: [
            made.make(o_scr.at[x % 2], outs[x]),
            made.make(do_scr.at[x], do_out.at[x]),
            made.make(st_scr.at[x], stat_out.at[x]),
            made.make(sum_scr.at[x], gq_out.at[x]),
        ]
        for x in range(lay.group)
    }

    def one(x, carry):
        slot = x % 2
        at_place(x, loads, wait_all)
        at_place(x, {p + 2: some for p, some in saves.items()}, lambda c: wait_all(c[:1]))
        mine = lay.query_block(w, jnp.bitwise_xor(u, x))
        live = count_ref[mine]

        def far(i, run):
            block = lay.table_block(list_ref[mine, i], u)

            @pl.when((block < first) | (block >= first + lay.group))
            def _():
                run(jnp.where(block < first, block, block - lay.group))

        for g in range(heads):
            m_scr[g] = spread(st_scr[x, :, g : g + 1], shape)

        def scores(i, c):
            def run(block):
                for g in range(heads):
                    s = dot(q_scr[x, :, COLS[g]], k_tab[block], NT)
                    s_scr[i - 1, g] = s
                    m_scr[g] = lane_max(m_scr[g], s)

            far(i, run)
            return c

        lax.fori_loop(1, live, scores, 0)
        stats = jnp.zeros(shape, jnp.float32)
        for g in range(heads):
            top = spread(jnp.max(m_scr[g], axis=1, keepdims=True), shape)
            old = spread(st_scr[x, :, g : g + 1], shape)
            total = spread(st_scr[x, :, heads + g : heads + g + 1], shape)
            fade = jnp.exp2((old - top) * EXP2_SCALE)
            o_acc[g, :, :HEAD_WIDTH] = sum_scr[x, :, COLS[g]] * fade
            o_acc[g, :, HEAD_WIDTH:] = total * fade
            m_scr[g] = top
            stats = jnp.where(lane == g, top, stats)

        def weigh(i, c):
            def run(block):
                v_ones = values_and_ones(v_tab[block])
                for g in range(heads):
                    e = score_weights(s_scr[i - 1, g], m_scr[g])
                    e_scr[i - 1, g] = e
                    o_acc[g] += dot(e, v_ones, NN)

            far(i, run)
            return c

        lax.fori_loop(1, live, weigh, 0)
        for g in range(heads):
            inverse = 1.0 / o_acc[g, :, HEAD_WIDTH:]
            attended = (o_acc[g, :, :HEAD_WIDTH] * inverse).astype(jnp.bfloat16)
            o_scr[slot, :, COLS[g]] = attended
            cot = do_scr[x, :, COLS[g]].astype(jnp.float32)
            delta = jnp.sum(attended.astype(jnp.float32) * cot, axis=1, keepdims=True)
            delta = delta * inverse
            m_scr[g] = delta
            stats = jnp.where(lane == heads + g, delta, stats)
            do_scr[x, :, COLS[g]] = (cot * inverse).astype(jnp.bfloat16)
        st_scr[x] = stats
        sum_scr[x] = jnp.zeros(sum_scr.shape[1:], jnp.float32)

        def grads(i, c):
            def run(block):
                dk, dv = None, None
                for g in range(heads):
                    cot = do_scr[x, :, COLS[g]]
                    e = e_scr[i - 1, g]
                    ds = score_grads(e, cot, v_tab[block], m_scr[g])
                    sum_scr[x, :, COLS[g]] += dot(ds, k_tab[block], NN)
                    dk_g = dot(ds, q_scr[x, :, COLS[g]], TN)
                    dv_g = dot(e, cot, TN)
                    dk = dk_g if dk is None else dk + dk_g
                    dv = dv_g if dv is None else dv + dv_g
                dk_acc[block] += dk
                dv_acc[block] += dv

            far(i, run)
            return c

        lax.fori_loop(1, live, grads, 0)
        at_place(x, saves, start_all)
        return carry

    lax.fori_loop(0, lay.group, one, 0)

    def narrow(b, carry):
        k_tab[b] = (dk_acc[b] * SCORE_SCALE).astype(jnp.bfloat16)
        v_tab[b] = dv_acc[b].astype(jnp.bfloat16)
        return carry

    lax.fori_loop(0, k_tab.shape[0], narrow, 0)
    guarded = far_copies(to_below, to_above, False)
    start_guarded(guarded)
    start_guarded(guarded, wait_all)
    for x, some in saves.items():
        wait_all(some if x >= lay.group - 2 else some[1:])


def near_kernel(lay, places, begin, end, list_ref, count_ref, where_ref, *refs):
    refs = list(refs)

    def take(n):
        taken = refs[:n]
        del refs[:n]
        return taken

    near = lay.per_block - 1
    raw = take(1 if begin else 0)
    slabs = take(len(places) - len(raw))
    do_in, stat_in, gq_in = take(3)
    own_table, below, above = take(1)[0], take(near), take(near)
    sums_in = [] if begin else take(2)
    if end:
        take(2 * near)
    outs = take(len(places))
    if end:
        own_sums, to_below, to_above = take(1)[0], take(near), take(near)
    else:
        sums_out = take(2)
    q_scr, do_scr, st_scr, gq_acc, k_tab, v_tab, dk_acc, dv_acc, m_scr, d_scr, sems = refs
    u, w = where_ref[0], where_ref[1]
    heads = GROUP_WIDTH
    made = Copies(sems)
    first = lay.place(w)[0]

    def is_near(valid, plane):
        return valid & (lay.place(plane)[0] == first)

    copies, guarded = near_tables(lay, made, w, (k_tab, v_tab), own_table, below, above)
    loads = {}
    for n, x in enumerate(places):
        if x == 0:
            src = raw[0].at[:, columns(u * heads, heads)]
        else:
            src = slabs[n - len(raw)]
        loads[n] = [
            made.make(src, q_scr.at[n]),
            made.make(do_in.at[x], do_scr.at[n]),
            made.make(stat_in.at[x], st_scr.at[n]),
            made.make(gq_in.at[x], gq_acc.at[n]),
        ]
    if not begin:
        copies += [made.make(sums_in[0], dk_acc), made.make(sums_in[1], dv_acc)]
    start_all(copies)
    start_guarded(guarded)
    for some in loads.values():
        start_all(some)
    if begin:
        dk_acc[...] = jnp.zeros_like(dk_acc)
        dv_acc[...] = jnp.zeros_like(dv_acc)
    wait_all(copies)
    start_guarded(guarded, wait_all)
    saves = {n: [made.make(q_scr.at[n], outs[n])] for n in loads}

    def one(n, carry):
        at_place(n, loads, wait_all)
        mine = lay.query_block(w, jnp.bitwise_xor(u, n + places[0]))
        for g in range(heads):
            m_scr[g] = jnp.broadcast_to(st_scr[n, :, g : g + 1], m_scr.shape[1:])
            d_scr[g] = jnp.broadcast_to(
                st_scr[n, :, heads + g : heads + g + 1], d_scr.shape[1:]
            )

        def grads(i, c):
            block = lay.table_block(list_ref[mine, i], u) - first

            @pl.when((block >= 0) & (block < lay.group))
            def _():
                dk, dv = None, None
                for g in range(heads):
                    q, cot = q_scr[n, :, COLS[g]], do_scr[n, :, COLS[g]]
                    e = score_weights(dot(q, k_tab[block], NT), m_scr[g])
                    ds = score_grads(e, cot, v_tab[block], d_scr[g])
                    gq_acc[n, :, COLS[g]] += dot(ds, k_tab[block], NN)
                    dk_g = dot(ds, q, TN)
                    dv_g = dot(e, cot, TN)
                    dk = dk_g if dk is None else dk + dk_g
                    dv = dv_g if dv is None else dv + dv_g
                dk_acc[block] += dk
                dv_acc[block] += dv

            return c

        lax.fori_loop(0, count_ref[mine], grads, 0)
        for g in range(heads):
            q_scr[n, :, COLS[g]] = (gq_acc[n, :, COLS[g]] * SCORE_SCALE).astype(jnp.bfloat16)
        at_place(n, saves, start_all)
        return carry

    lax.fori_loop(0, len(places), one, 0)
    if end:

        def narrow(b, carry):
            k_tab[b] = (dk_acc[b] * SCORE_SCALE).astype(jnp.bfloat16)
            v_tab[b] = dv_acc[b].astype(jnp.bfloat16)
            return carry

        lax.fori_loop(0, lay.group, narrow, 0)
        copies = table_copies(lay, made, w, (k_tab, v_tab), own_sums, False, first)
        guarded = [
            (is_near(valid, plane), table_copies(lay, made, plane, (k_tab, v_tab), t, False, first))
            for valid, plane, t in offsets(lay, w, to_below, to_above)
        ]
    else:
        copies = [made.make(dk_acc, sums_out[0]), made.make(dv_acc, sums_out[1])]
        guarded = []
    start_all(copies)
    start_guarded(guarded)
    start_guarded(guarded, wait_all)
    wait_all(copies)
    for some in saves.values():
        wait_all(some)


def kernel_call(kernel, lay, scalars, operands, out_shape, scratch, tiles, aliases):
    return pl.pallas_call(
        kernel,
        out_shape=out_shape,
        grid_spec=pltpu.PrefetchScalarGridSpec(
            num_scalar_prefetch=len(scalars),
            grid=(1,),
            in_specs=[ANY] * len(operands),
            out_specs=[ANY] * len(out_shape),
            scratch_shapes=scratch,
        ),
        input_output_aliases=aliases,
        compiler_params=pltpu.CompilerParams(vmem_limit_bytes=VMEM_BYTES),
        cost_estimate=pl.CostEstimate(
            flops=tiles * 24 * lay.tokens * BLOCK_TOKENS * HEAD_WIDTH * GROUP_WIDTH,
            transcendentals=tiles * lay.tokens * BLOCK_TOKENS * GROUP_WIDTH,
            bytes_accessed=16 * 1024 * 1024,
        ),
    )(*scalars, *operands)


def near_forward(lay, scalars, raw, slabs, own_table, below, above):
    bf, f32 = jnp.bfloat16, jnp.float32
    width = GROUP_WIDTH * HEAD_WIDTH
    near = (lay.group, BLOCK_TOKENS, HEAD_WIDTH)
    own = (lay.group, lay.tokens, width)
    most = scalars[0].shape[1]
    n = lay.per_block - 1
    stats = (lay.group, lay.tokens, HEAD_WIDTH)
    scratch = [
        pltpu.VMEM(own, bf),
        *[pltpu.VMEM(near, bf)] * 2,
        pltpu.VMEM((most, GROUP_WIDTH, lay.tokens, BLOCK_TOKENS), f32),
        pltpu.VMEM((GROUP_WIDTH, lay.tokens, HEAD_WIDTH), f32),
        pltpu.VMEM((GROUP_WIDTH, lay.tokens, 2 * HEAD_WIDTH), f32),
        pltpu.VMEM((2, lay.tokens, width), f32),
        pltpu.VMEM(stats, f32),
        pltpu.SemaphoreType.DMA((3 * lay.group + 4 * n + 2,)),
    ]
    out_shape = [jax.ShapeDtypeStruct(own, f32), jax.ShapeDtypeStruct(stats, f32)]
    operands = [raw, *slabs, own_table, *below[:n], *above[:n]]
    return kernel_call(
        functools.partial(near_forward_kernel, lay),
        lay, scalars, operands, out_shape, scratch, lay.group, {},
    )


def forward(lay, scalars, raw, q_slabs, do_slabs, begun, below, above):
    bf, f32 = jnp.bfloat16, jnp.float32
    width = GROUP_WIDTH * HEAD_WIDTH
    far_tables = (lay.blocks - lay.group, BLOCK_TOKENS, HEAD_WIDTH)
    own = (lay.group, lay.tokens, width)
    most = scalars[0].shape[1]
    tile = (GROUP_WIDTH, lay.tokens, BLOCK_TOKENS)
    far = 2 * (lay.line - 1)
    stats = (lay.group, lay.tokens, HEAD_WIDTH)
    scratch = [
        *[pltpu.VMEM(own, bf)] * 2,
        pltpu.VMEM(own, f32),
        *[pltpu.VMEM(far_tables, bf)] * 2,
        *[pltpu.VMEM(far_tables, f32)] * 2,
        pltpu.VMEM((most - 1, *tile), f32),
        pltpu.VMEM((most - 1, *tile), bf),
        pltpu.VMEM((GROUP_WIDTH, lay.tokens, HEAD_WIDTH), f32),
        pltpu.VMEM((GROUP_WIDTH, lay.tokens, 2 * HEAD_WIDTH), f32),
        pltpu.VMEM((2, lay.tokens, width), bf),
        pltpu.VMEM(stats, f32),
        pltpu.SemaphoreType.DMA((8 * lay.group + 4 * far,)),
    ]
    table = (2, lay.group, lay.tokens, HEAD_WIDTH)
    out_shape = [bf16(lay.tokens, width)] * lay.group
    out_shape += [bf16(*own), jax.ShapeDtypeStruct(stats, f32), jax.ShapeDtypeStruct(own, f32)]
    out_shape += [bf16(*table)] * far
    operands = [*raw, *q_slabs, *do_slabs, *begun, *below, *above]
    outs = kernel_call(
        functools.partial(forward_kernel, lay),
        lay, scalars, operands, out_shape, scratch, lay.group * most // 4, {},
    )
    n = lay.group
    return outs[:n], outs[n : n + 3], outs[n + 3 : n + 2 + lay.line], outs[n + 2 + lay.line :]


def near_grads(lay, scalars, places, raw, slabs, carried, own_table, below, above, sums, to_below, to_above):
    bf, f32 = jnp.bfloat16, jnp.float32
    width = GROUP_WIDTH * HEAD_WIDTH
    n, near = len(places), lay.per_block - 1
    begin, end = places[0] == 0, places[-1] == lay.group - 1
    whole = (lay.group, BLOCK_TOKENS, HEAD_WIDTH)
    scratch = [
        *[pltpu.VMEM((n, lay.tokens, width), bf)] * 2,
        pltpu.VMEM((n, lay.tokens, HEAD_WIDTH), f32),
        pltpu.VMEM((n, lay.tokens, width), f32),
        *[pltpu.VMEM(whole, bf)] * 2,
        *[pltpu.VMEM(whole, f32)] * 2,
        *[pltpu.VMEM((GROUP_WIDTH, lay.tokens, HEAD_WIDTH), f32)] * 2,
        pltpu.SemaphoreType.DMA((5 * n + 8 * near + 8,)),
    ]
    operands = [*(raw if begin else []), *slabs, *carried, own_table, *below[:near], *above[:near], *sums]
    out_shape, aliases = [bf16(lay.tokens, width)] * n, {}
    if end:
        out_shape.append(bf16(2, lay.group, lay.tokens, HEAD_WIDTH))
        for array in (*to_below[:near], *to_above[:near]):
            aliases[len(scalars) + len(operands)] = len(out_shape)
            operands.append(array)
            out_shape.append(bf16(*array.shape))
    else:
        out_shape += [jax.ShapeDtypeStruct(whole, f32)] * 2
    most = scalars[0].shape[1]
    outs = kernel_call(
        functools.partial(near_kernel, lay, places, begin, end),
        lay, scalars, operands, out_shape, scratch, n * most // 4, aliases,
    )
    return outs[:n], outs[n:]


def add(a, b):
    return (a.astype(jnp.float32) + b.astype(jnp.float32)).astype(jnp.bfloat16)


def shards(ctx_size, head_size, queries, keys, values, cotangent, block_list, block_count):
    lay = Layout(ctx_size, head_size, queries.shape[0])
    ctx_rank, head_rank = lax.axis_index("ctx"), lax.axis_index("head")
    u = lax.rem(ctx_rank, lay.group)
    w = ctx_rank // lay.group * lay.heads + head_rank
    where = jnp.stack([u, w]).astype(jnp.int32)
    n = lay.line

    local, *sent = pack(lay, where, (keys, values), 1, range(lay.group))
    came = [lay.swap(s, x) for x, s in zip(lay.others, sent)]
    own_table = collect(lay, [local, *came])
    below, above = [own_table], [own_table]
    for k in range(1, n):
        below.append(lay.shift(below[-1], range(k - 1, n - 1), 1))
        above.append(lay.shift(above[-1], range(1, n - k + 1), -1))
    scalars = (block_list, block_count, where)
    raw = (queries, cotangent)
    sent = pack_one(lay, where, queries, GROUP_WIDTH)
    slabs = [lay.swap(s, x) for x, s in zip(lay.others, sent)]
    sent = pack_one(lay, where, cotangent, GROUP_WIDTH)
    do_slabs = [lay.swap(s, x) for x, s in zip(lay.others, sent)]
    begun = near_forward(lay, scalars, queries, slabs, own_table, below[1:], above[1:])
    outs, carried, to_below, to_above = forward(
        lay, scalars, raw, slabs, do_slabs, begun, below[1:], above[1:]
    )
    attended = [outs[0], *[lay.swap(s, x) for x, s in zip(lay.others, outs[1:])]]
    up, down = to_above[n - 2], to_below[n - 2]
    shares = [list(range(i, i + lay.group // 2)) for i in range(0, lay.group, lay.group // 2)]
    grad_query, sums = [], []
    for k in range(n - 1, 0, -1):
        step = n - k
        up = lay.shift(up, range(0, n - k), 1)
        down = lay.shift(down, range(k, n), -1)
        if step <= len(shares):
            places = shares[step - 1]
            outs, sums = near_grads(
                lay, scalars, places, raw[:1],
                [slabs[x - 1] for x in places if x],
                carried, own_table, below[1:], above[1:], sums, to_below, to_above,
            )
            grad_query += [lay.swap(s, x) if x else s for x, s in zip(places, outs)]
            if step == len(shares):
                near = lay.per_block - 1
                own_sums = sums[0]
                to_below = [*sums[1 : 1 + near], *to_below[near:]]
                to_above = [*sums[1 + near :], *to_above[near:]]
        if k > 1:
            up, down = add(up, to_above[k - 2]), add(down, to_below[k - 2])
    local, *sent = split(lay, [own_sums, up, down])
    came = [lay.swap(s, x) for x, s in zip(lay.others, sent)]
    key_grad, value_grad = unpack(lay, where, [[local, *came]], 1)
    attn_out = unpack(lay, where, [attended], GROUP_WIDTH)[0]
    grad_q = unpack(lay, where, [grad_query], GROUP_WIDTH)[0]
    return attn_out, grad_q, key_grad, value_grad


def solution(mesh):
    placed = P(("ctx", "head"), None)

    def body(*args):
        return shards(mesh.shape["ctx"], mesh.shape["head"], *args)

    return jax.shard_map(
        body,
        mesh=mesh,
        in_specs=(placed,) * 4 + (P(), P()),
        out_specs=(placed,) * 4,
        check_vma=False,
    )
```

profile of v0, /device:TPU:1, one launch (start us, length us, event | category | flops | bytes accessed | tf_op | source)
XLA Modules:
  0.0 406.9 jit_solution(18145731631465038632)
XLA Ops:
  13.8 6.6 %collective-permute-done.18.refs_5_ = bf16[2,256,128]{2,1,0:T(8,128)(2,1)S(1)} collective-permute-done((bf16[2,256,128]{2,1,0:T(8,128)(2,1)}, bf16[2,256,128]{2,1,0:T(8,128)(2,1)S(1)}, u32[]{:S(2)}, u32[]{:S(2)}) %collective-permute-start.18) | collective-permute-done | bytes 131104 | tf_op jit(solution)/shard_map/ppermute | solution.py:79
  24.8 5.0 %collective-permute-start.21 = (bf16[2,8,256,128]{3,2,1,0:T(8,128)(2,1)}, bf16[2,8,256,128]{3,2,1,0:T(8,128)(2,1)}, u32[]{:S(2)}, u32[]{:S(2)}) collective-permute-start(bf16[2,8,256,128]{3,2,1,0:T(8,128)(2,1)} %shard_map.96.refs_8_.refs_7_), channel_id=1, source_target_pairs={{0,1},{4,5},{8,9},{12,13},{16,17},{20,21},{24,25},{28,29},{1,2},{5... | collective-permute-start | bytes 3145736 | tf_op jit(solution)/shard_map/ppermute | solution.py:85
  29.9 3.5 shard_map.94
  35.7 3.5 shard_map.93
  40.8 4.0 collective-permute-done.8.refs_10_
  46.3 4.2 %collective-permute-done.22.refs_10_.refs_21_.refs_9_ = bf16[2,8,256,128]{3,2,1,0:T(8,128)(2,1)S(1)} collective-permute-done((bf16[2,8,256,128]{3,2,1,0:T(8,128)(2,1)}, bf16[2,8,256,128]{3,2,1,0:T(8,128)(2,1)S(1)}, u32[]{:S(2)}, u32[]{:S(2)}) %collective-permute-start.22) | collective-permute-done | bytes 1048608 | tf_op jit(solution)/shard_map/ppermute | solution.py:85
  57.4 6.6 %collective-permute-done.1.refs_2_.refs_3_ = bf16[256,768]{1,0:T(8,128)(2,1)S(1)} collective-permute-done((bf16[256,768]{1,0:T(8,128)(2,1)}, bf16[256,768]{1,0:T(8,128)(2,1)S(1)}, u32[]{:S(2)}, u32[]{:S(2)}) %collective-permute-start.1) | collective-permute-done | bytes 393248 | tf_op jit(solution)/shard_map/ppermute | solution.py:79
  63.9 3.8 collective-permute-start.4
  67.7 5.7 %collective-permute-done.2.refs_3_.refs_4_ = bf16[256,768]{1,0:T(8,128)(2,1)S(1)} collective-permute-done((bf16[256,768]{1,0:T(8,128)(2,1)}, bf16[256,768]{1,0:T(8,128)(2,1)S(1)}, u32[]{:S(2)}, u32[]{:S(2)}) %collective-permute-start.2) | collective-permute-done | bytes 393248 | tf_op jit(solution)/shard_map/ppermute | solution.py:79
  79.1 7.4 %collective-permute-done.5.refs_6_.refs_7_.refs_2_ = bf16[256,768]{1,0:T(8,128)(2,1)S(1)} collective-permute-done((bf16[256,768]{1,0:T(8,128)(2,1)}, bf16[256,768]{1,0:T(8,128)(2,1)S(1)}, u32[]{:S(2)}, u32[]{:S(2)}) %collective-permute-start.5) | collective-permute-done | bytes 393248 | tf_op jit(solution)/shard_map/ppermute | solution.py:79
  88.7 6.2 %collective-permute-done.6.refs_7_.refs_8_.refs_3_ = bf16[256,768]{1,0:T(8,128)(2,1)S(1)} collective-permute-done((bf16[256,768]{1,0:T(8,128)(2,1)}, bf16[256,768]{1,0:T(8,128)(2,1)S(1)}, u32[]{:S(2)}, u32[]{:S(2)}) %collective-permute-start.6) | collective-permute-done | bytes 393248 | tf_op jit(solution)/shard_map/ppermute | solution.py:79
  100.7 35.2 %shard_map.97 = (f32[8,256,768]{2,1,0:T(8,128)}, f32[8,256,128]{2,1,0:T(8,128)}) custom-call(s32[16,8]{1,0:T(8,128)} %copy.13.list_ref, s32[16]{0:T(128)} %count_ref.7, s32[2]{0:T(128)} %pad_add_fusion.refs_0_.where_ref, bf16[256,6144]{1,0:T(8,128)(2,1)} %refs_0_.5, bf16[256,768]{1,0:T(8,128)(2,1)} %copy-done.27, bf16[256,768]{1,0:T(8,128)(2,1)} %copy-done.33, ...), custom_call_target="tpu_custom_call" | custom-call | flops 19327352832 | bytes 16777216 | tf_op jit(solution)/shard_map/pallas_call | solution.py:646
  135.9 38.6 %shard_map.98 = (bf16[256,768]{1,0:T(8,128)(2,1)}, bf16[256,768]{1,0:T(8,128)(2,1)}, bf16[256,768]{1,0:T(8,128)(2,1)}, bf16[256,768]{1,0:T(8,128)(2,1)}, bf16[25...) custom-call(s32[16,8]{1,0:T(8,128)} %copy.13.list_ref, ...), custom_call_target="tpu_custom_call" | custom-call | flops 38654705664 | bytes 16777216 | tf_op jit(solution)/shard_map/pallas_call | solution.py:646
  176.7 10.0 %collective-permute-start.41 = (bf16[2,8,256,128]{3,2,1,0:T(8,128)(2,1)}, bf16[2,8,256,128]{3,2,1,0:T(8,128)(2,1)}, u32[]{:S(2)}, u32[]{:S(2)}) collective-permute-start(bf16[2,8,256,128]{3,2,1,0:T(8,128)(2,1)} %get-tuple-element.116), channel_id=1, source_target_pairs={{0,1},{4,5},{8,9},{12,13},{16,17},{20,21},{24,25},{28,29}} | collective-permute-start | bytes 3145736 | tf_op jit(solution)/shard_map/ppermute | solution.py:85
  188.4 45.3 %shard_map.100 = (bf16[256,768]{1,0:T(8,128)(2,1)}, bf16[256,768]{1,0:T(8,128)(2,1)}, bf16[256,768]{1,0:T(8,128)(2,1)}, bf16[256,768]{1,0:T(8,128)(2,1)}, f32[8,...) custom-call(s32[16,8]{1,0:T(8,128)} %copy.13.list_ref, s32[16]{0:T(128)} %count_ref.7, s32[2]{0:T(128)} %pad_add_fusion.refs_0_.where_ref, ...), custom_call_target="tpu_custom_call" | custom-call | flops 19327352832 | bytes 16777216 | tf_op jit(solution)/shard_map/pallas_call | solution.py:646
  241.8 34.4 %shard_map.101 = (bf16[256,768]{1,0:T(8,128)(2,1)}, bf16[256,768]{1,0:T(8,128)(2,1)}, bf16[256,768]{1,0:T(8,128)(2,1)}, bf16[256,768]{1,0:T(8,128)(2,1)}, bf16[2...) custom-call(s32[16,8]{1,0:T(8,128)} %copy.13.list_ref, ...), custom_call_target="tpu_custom_call", output_to_operand_aliasing={{5}: (15, {}), {6}: (16, {})} | custom-call | flops 19327352832 | bytes 16777216 | tf_op jit(solution)/shard_map/pallas_call | solution.py:646
  282.6 30.0 %collective-permute-start.30 = (bf16[256,768]{1,0:T(8,128)(2,1)S(1)}, bf16[256,768]{1,0:T(8,128)(2,1)S(1)}, u32[]{:S(2)}, u32[]{:S(2)}) collective-permute-start(bf16[256,768]{1,0:T(8,128)(2,1)S(1)} %copy-done.40), channel_id=1, source_target_pairs={{0,16},{4,20},{8,24},{12,28},{16,0},{20,4},{24,8},{28,12},{1,17},{... | collective-permute-start | bytes 1179656 | tf_op jit(solution)/shard_map/ppermute | solution.py:79
  315.6 14.4 %collective-permute-done.30.refs_5_ = bf16[256,768]{1,0:T(8,128)(2,1)S(1)} collective-permute-done((bf16[256,768]{1,0:T(8,128)(2,1)S(1)}, bf16[256,768]{1,0:T(8,128)(2,1)S(1)}, u32[]{:S(2)}, u32[]{:S(2)}) %collective-permute-start.30) | collective-permute-done | bytes 393248 | tf_op jit(solution)/shard_map/ppermute | solution.py:79
  330.1 4.1 %collective-permute-start.33 = (bf16[256,768]{1,0:T(8,128)(2,1)S(1)}, bf16[256,768]{1,0:T(8,128)(2,1)S(1)}, u32[]{:S(2)}, u32[]{:S(2)}) collective-permute-start(bf16[256,768]{1,0:T(8,128)(2,1)S(1)} %copy-done.34), channel_id=1, source_target_pairs={{0,28},{4,24},{8,20},{12,16},{16,12},{20,8},{24,4},{28,0},{1,29},{... | collective-permute-start | bytes 1179656 | tf_op jit(solution)/shard_map/ppermute | solution.py:79
  334.2 13.0 %collective-permute-done.31.refs_6_ = bf16[256,768]{1,0:T(8,128)(2,1)S(1)} collective-permute-done((bf16[256,768]{1,0:T(8,128)(2,1)S(1)}, bf16[256,768]{1,0:T(8,128)(2,1)S(1)}, u32[]{:S(2)}, u32[]{:S(2)}) %collective-permute-start.31) | collective-permute-done | bytes 393248 | tf_op jit(solution)/shard_map/ppermute | solution.py:79
  350.9 6.8 %collective-permute-done.35.refs_3_ = bf16[256,768]{1,0:T(8,128)(2,1)S(1)} collective-permute-done((bf16[256,768]{1,0:T(8,128)(2,1)S(1)}, bf16[256,768]{1,0:T(8,128)(2,1)S(1)}, u32[]{:S(2)}, u32[]{:S(2)}) %collective-permute-start.35) | collective-permute-done | bytes 393248 | tf_op jit(solution)/shard_map/ppermute | solution.py:79
  369.1 18.6 %collective-permute-done.38.refs_6_ = bf16[256,768]{1,0:T(8,128)(2,1)} collective-permute-done((bf16[256,768]{1,0:T(8,128)(2,1)}, bf16[256,768]{1,0:T(8,128)(2,1)}, u32[]{:S(2)}, u32[]{:S(2)}) %collective-permute-start.38) | collective-permute-done | bytes 393248 | tf_op jit(solution)/shard_map/ppermute | solution.py:79
  393.6 4.3 %shard_map.99 = bf16[256,6144]{1,0:T(8,128)(2,1)} custom-call(s32[2]{0:T(128)} %pad_add_fusion.refs_0_.where_ref, bf16[256,768]{1,0:T(8,128)(2,1)} %get-tuple-element.92.refs_1_, bf16[256,768]{1,0:T(8,128)(2,1)} %copy-done.5, bf16[256,768]{1,0:T(8,128)(2,1)} %copy-done.6, bf16[256,768]{1,0:T(8,128)(2,1)} %collective-permute-done.29.refs_4_, ...), custom_call_target="tpu_custom_call" | custom-call | bytes 6291456 | tf_op jit(solution)/shard_map/pallas_call | solution.py:108
  397.9 4.3 %shard_map.102 = bf16[256,6144]{1,0:T(8,128)(2,1)} custom-call(s32[2]{0:T(128)} %pad_add_fusion.refs_0_.where_ref, bf16[256,768]{1,0:T(8,128)(2,1)} %get-tuple-element.103.refs_1_, bf16[256,768]{1,0:T(8,128)(2,1)} %copy-done.11, bf16[256,768]{1,0:T(8,128)(2,1)} %copy-done.12, bf16[256,768]{1,0:T(8,128)(2,1)} %collective-permute-done.36.refs_4_, ...), custom_call_target="tpu_custom_call" | custom-call | bytes 6291456 | tf_op jit(solution)/shard_map/pallas_call | solution.py:108
  (188 shorter events, 89.7 us)
Async XLA Ops:
  23.5 27.0 %collective-permute-start.22 = (bf16[2,8,256,128]{3,2,1,0:T(8,128)(2,1)}, bf16[2,8,256,128]{3,2,1,0:T(8,128)(2,1)S(1)}, u32[]{:S(2)}, u32[]{:S(2)}) collective-permute-start(bf16[2,8,256,128]{3,2,1,0:T(8,128)(2,1)} %shard_map.96.refs_8_.refs_7_), channel_id=1, source_target_pairs={{1,0},{5,4},{9,8},{13,12},{17,16},{21,20},{25,24},{29,28},{2,1},{6... | collective-permute-start | bytes 3145736 | tf_op jit(solution)/shard_map/ppermute | solution.py:85
  24.8 27.0 %collective-permute-start.21 = (bf16[2,8,256,128]{3,2,1,0:T(8,128)(2,1)}, bf16[2,8,256,128]{3,2,1,0:T(8,128)(2,1)}, u32[]{:S(2)}, u32[]{:S(2)}) collective-permute-start(bf16[2,8,256,128]{3,2,1,0:T(8,128)(2,1)} %shard_map.96.refs_8_.refs_7_), channel_id=1, source_target_pairs={{0,1},{4,5},{8,9},{12,13},{16,17},{20,21},{24,25},{28,29},{1,2},{5... | collective-permute-start | bytes 3145736 | tf_op jit(solution)/shard_map/ppermute | solution.py:85
  50.5 47.2 %collective-permute-start.25 = (bf16[2,8,256,128]{3,2,1,0:T(8,128)(2,1)S(1)}, bf16[2,8,256,128]{3,2,1,0:T(8,128)(2,1)}, u32[]{:S(2)}, u32[]{:S(2)}) collective-permute-start(bf16[2,8,256,128]{3,2,1,0:T(8,128)(2,1)S(1)} %collective-permute-done.22.refs_10_.refs_21_.refs_9_), channel_id=1, source_target_pairs={{1,0},{5,4},{9,8},{13,12},{17,16},{21,20},{25,24},{29,28},{2,1},{6... | collective-permute-start | bytes 3145736 | tf_op jit(solution)/shard_map/ppermute | solution.py:85
  51.8 47.2 %collective-permute-start.23 = (bf16[2,8,256,128]{3,2,1,0:T(8,128)(2,1)}, bf16[2,8,256,128]{3,2,1,0:T(8,128)(2,1)}, u32[]{:S(2)}, u32[]{:S(2)}) collective-permute-start(bf16[2,8,256,128]{3,2,1,0:T(8,128)(2,1)} %collective-permute-done.21.refs_9_.refs_18_.refs_8_), channel_id=1, source_target_pairs={{1,2},{5,6},{9,10},{13,14},{17,18},{21,22},{25,26},{29,30},{2,3},{... | collective-permute-start | bytes 3145736 | tf_op jit(solution)/shard_map/ppermute | solution.py:85
  77.7 58.2 %collective-permute-start.11 = (bf16[256,768]{1,0:T(8,128)(2,1)}, bf16[256,768]{1,0:T(8,128)(2,1)}, u32[]{:S(2)}, u32[]{:S(2)}) collective-permute-start(bf16[256,768]{1,0:T(8,128)(2,1)} %get-tuple-element.79), channel_id=1, source_target_pairs={{0,20},{4,16},{8,28},{12,24},{16,4},{20,0},{24,12},{28,8},{1,21},{... | collective-permute-start | bytes 1179656 | tf_op jit(solution)/shard_map/ppermute | solution.py:79
  86.5 49.4 %collective-permute-start.12 = (bf16[256,768]{1,0:T(8,128)(2,1)}, bf16[256,768]{1,0:T(8,128)(2,1)}, u32[]{:S(2)}, u32[]{:S(2)}) collective-permute-start(bf16[256,768]{1,0:T(8,128)(2,1)} %get-tuple-element.80), channel_id=1, source_target_pairs={{0,24},{4,28},{8,16},{12,20},{16,8},{20,12},{24,0},{28,4},{1,25},{... | collective-permute-start | bytes 1179656 | tf_op jit(solution)/shard_map/ppermute | solution.py:79
  94.9 41.0 %collective-permute-start.13 = (bf16[256,768]{1,0:T(8,128)(2,1)}, bf16[256,768]{1,0:T(8,128)(2,1)}, u32[]{:S(2)}, u32[]{:S(2)}) collective-permute-start(bf16[256,768]{1,0:T(8,128)(2,1)} %get-tuple-element.81), channel_id=1, source_target_pairs={{0,28},{4,24},{8,20},{12,16},{16,12},{20,8},{24,4},{28,0},{1,29},{... | collective-permute-start | bytes 1179656 | tf_op jit(solution)/shard_map/ppermute | solution.py:79
  97.7 38.2 %collective-permute-start.26 = (bf16[2,8,256,128]{3,2,1,0:T(8,128)(2,1)}, bf16[2,8,256,128]{3,2,1,0:T(8,128)(2,1)}, u32[]{:S(2)}, u32[]{:S(2)}) collective-permute-start(bf16[2,8,256,128]{3,2,1,0:T(8,128)(2,1)} %collective-permute-done.25.refs_22_), channel_id=1, source_target_pairs={{1,0},{5,4},{9,8},{13,12},{17,16},{21,20},{25,24},{29,28}} | collective-permute-start | bytes 3145736 | tf_op jit(solution)/shard_map/ppermute | solution.py:85
  99.0 36.9 %collective-permute-start.24 = (bf16[2,8,256,128]{3,2,1,0:T(8,128)(2,1)}, bf16[2,8,256,128]{3,2,1,0:T(8,128)(2,1)}, u32[]{:S(2)}, u32[]{:S(2)}) collective-permute-start(bf16[2,8,256,128]{3,2,1,0:T(8,128)(2,1)} %collective-permute-done.23.refs_19_), channel_id=1, source_target_pairs={{2,3},{6,7},{10,11},{14,15},{18,19},{22,23},{26,27},{30,31}} | collective-permute-start | bytes 3145736 | tf_op jit(solution)/shard_map/ppermute | solution.py:85
  174.5 108.0 %collective-permute-start.27 = (bf16[256,768]{1,0:T(8,128)(2,1)}, bf16[256,768]{1,0:T(8,128)(2,1)S(1)}, u32[]{:S(2)}, u32[]{:S(2)}) collective-permute-start(bf16[256,768]{1,0:T(8,128)(2,1)} %get-tuple-element.93), channel_id=1, source_target_pairs={{0,4},{4,0},{8,12},{12,8},{16,20},{20,16},{24,28},{28,24},{1,5},{5... | collective-permute-start | bytes 1179656 | tf_op jit(solution)/shard_map/ppermute | solution.py:79
  174.6 138.0 %collective-permute-start.28 = (bf16[256,768]{1,0:T(8,128)(2,1)}, bf16[256,768]{1,0:T(8,128)(2,1)S(1)}, u32[]{:S(2)}, u32[]{:S(2)}) collective-permute-start(bf16[256,768]{1,0:T(8,128)(2,1)} %get-tuple-element.94), channel_id=1, source_target_pairs={{0,8},{4,12},{8,0},{12,4},{16,24},{20,28},{24,16},{28,20},{1,9},{5... | collective-permute-start | bytes 1179656 | tf_op jit(solution)/shard_map/ppermute | solution.py:79
  174.9 138.0 %collective-permute-start.29 = (bf16[256,768]{1,0:T(8,128)(2,1)}, bf16[256,768]{1,0:T(8,128)(2,1)}, u32[]{:S(2)}, u32[]{:S(2)}) collective-permute-start(bf16[256,768]{1,0:T(8,128)(2,1)} %get-tuple-element.95), channel_id=1, source_target_pairs={{0,12},{4,8},{8,4},{12,0},{16,28},{20,24},{24,20},{28,16},{1,13},{... | collective-permute-start | bytes 1179656 | tf_op jit(solution)/shard_map/ppermute | solution.py:79
  176.7 57.0 %collective-permute-start.41 = (bf16[2,8,256,128]{3,2,1,0:T(8,128)(2,1)}, bf16[2,8,256,128]{3,2,1,0:T(8,128)(2,1)}, u32[]{:S(2)}, u32[]{:S(2)}) collective-permute-start(bf16[2,8,256,128]{3,2,1,0:T(8,128)(2,1)} %get-tuple-element.116), channel_id=1, source_target_pairs={{0,1},{4,5},{8,9},{12,13},{16,17},{20,21},{24,25},{28,29}} | collective-permute-start | bytes 3145736 | tf_op jit(solution)/shard_map/ppermute | solution.py:85
  186.7 51.9 %collective-permute-start.44 = (bf16[2,8,256,128]{3,2,1,0:T(8,128)(2,1)}, bf16[2,8,256,128]{3,2,1,0:T(8,128)(2,1)}, u32[]{:S(2)}, u32[]{:S(2)}) collective-permute-start(bf16[2,8,256,128]{3,2,1,0:T(8,128)(2,1)} %get-tuple-element.119), channel_id=1, source_target_pairs={{3,2},{7,6},{11,10},{15,14},{19,18},{23,22},{27,26},{31,30}} | collective-permute-start | bytes 3145736 | tf_op jit(solution)/shard_map/ppermute | solution.py:85
  236.3 39.9 %collective-permute-start.42 = (bf16[2,8,256,128]{3,2,1,0:T(8,128)(2,1)}, bf16[2,8,256,128]{3,2,1,0:T(8,128)(2,1)}, u32[]{:S(2)}, u32[]{:S(2)}) collective-permute-start(bf16[2,8,256,128]{3,2,1,0:T(8,128)(2,1)} %add_convert_fusion.3), channel_id=1, source_target_pairs={{0,1},{4,5},{8,9},{12,13},{16,17},{20,21},{24,25},{28,29},{1,2},{5... | collective-permute-start | bytes 3145736 | tf_op jit(solution)/shard_map/ppermute | solution.py:85
  240.2 39.6 %collective-permute-start.45 = (bf16[2,8,256,128]{3,2,1,0:T(8,128)(2,1)S(1)}, bf16[2,8,256,128]{3,2,1,0:T(8,128)(2,1)}, u32[]{:S(2)}, u32[]{:S(2)}) collective-permute-start(bf16[2,8,256,128]{3,2,1,0:T(8,128)(2,1)S(1)} %add_convert_fusion.1), channel_id=1, source_target_pairs={{2,1},{6,5},{10,9},{14,13},{18,17},{22,21},{26,25},{30,29},{3,2},{... | collective-permute-start | bytes 3145736 | tf_op jit(solution)/shard_map/ppermute | solution.py:85
  278.2 82.9 %collective-permute-start.43 = (bf16[2,8,256,128]{3,2,1,0:T(8,128)(2,1)S(1)}, bf16[2,8,256,128]{3,2,1,0:T(8,128)(2,1)S(1)}, u32[]{:S(2)}, u32[]{:S(2)}) collective-permute-start(bf16[2,8,256,128]{3,2,1,0:T(8,128)(2,1)S(1)} %add_convert_fusion.2), channel_id=1, source_target_pairs={{0,1},{4,5},{8,9},{12,13},{16,17},{20,21},{24,25},{28,29},{1,2},{5... | collective-permute-start | bytes 3145736 | tf_op jit(solution)/shard_map/ppermute | solution.py:85
  281.2 80.8 %collective-permute-start.46 = (bf16[2,8,256,128]{3,2,1,0:T(8,128)(2,1)S(1)}, bf16[2,8,256,128]{3,2,1,0:T(8,128)(2,1)S(1)}, u32[]{:S(2)}, u32[]{:S(2)}) collective-permute-start(bf16[2,8,256,128]{3,2,1,0:T(8,128)(2,1)S(1)} %add_convert_fusion), channel_id=1, source_target_pairs={{1,0},{5,4},{9,8},{13,12},{17,16},{21,20},{25,24},{29,28},{2,1},{6... | collective-permute-start | bytes 3145736 | tf_op jit(solution)/shard_map/ppermute | solution.py:85
  282.6 47.5 %collective-permute-start.30 = (bf16[256,768]{1,0:T(8,128)(2,1)S(1)}, bf16[256,768]{1,0:T(8,128)(2,1)S(1)}, u32[]{:S(2)}, u32[]{:S(2)}) collective-permute-start(bf16[256,768]{1,0:T(8,128)(2,1)S(1)} %copy-done.40), channel_id=1, source_target_pairs={{0,16},{4,20},{8,24},{12,28},{16,0},{20,4},{24,8},{28,12},{1,17},{... | collective-permute-start | bytes 1179656 | tf_op jit(solution)/shard_map/ppermute | solution.py:79
  312.6 34.7 %collective-permute-start.31 = (bf16[256,768]{1,0:T(8,128)(2,1)S(1)}, bf16[256,768]{1,0:T(8,128)(2,1)S(1)}, u32[]{:S(2)}, u32[]{:S(2)}) collective-permute-start(bf16[256,768]{1,0:T(8,128)(2,1)S(1)} %copy-done.39), channel_id=1, source_target_pairs={{0,20},{4,16},{8,28},{12,24},{16,4},{20,0},{24,12},{28,8},{1,21},{... | collective-permute-start | bytes 1179656 | tf_op jit(solution)/shard_map/ppermute | solution.py:79
  313.0 34.3 %collective-permute-start.32 = (bf16[256,768]{1,0:T(8,128)(2,1)S(1)}, bf16[256,768]{1,0:T(8,128)(2,1)S(1)}, u32[]{:S(2)}, u32[]{:S(2)}) collective-permute-start(bf16[256,768]{1,0:T(8,128)(2,1)S(1)} %copy-done.38), channel_id=1, source_target_pairs={{0,24},{4,28},{8,16},{12,20},{16,8},{20,12},{24,0},{28,4},{1,25},{... | collective-permute-start | bytes 1179656 | tf_op jit(solution)/shard_map/ppermute | solution.py:79
  357.7 30.0 %collective-permute-start.38 = (bf16[256,768]{1,0:T(8,128)(2,1)}, bf16[256,768]{1,0:T(8,128)(2,1)}, u32[]{:S(2)}, u32[]{:S(2)}) collective-permute-start(bf16[256,768]{1,0:T(8,128)(2,1)} %get-tuple-element.112), channel_id=1, source_target_pairs={{0,20},{4,16},{8,28},{12,24},{16,4},{20,0},{24,12},{28,8},{1,21},{... | collective-permute-start | bytes 1179656 | tf_op jit(solution)/shard_map/ppermute | solution.py:79
  361.1 28.0 %collective-permute-start.39 = (bf16[256,768]{1,0:T(8,128)(2,1)}, bf16[256,768]{1,0:T(8,128)(2,1)}, u32[]{:S(2)}, u32[]{:S(2)}) collective-permute-start(bf16[256,768]{1,0:T(8,128)(2,1)} %get-tuple-element.113), channel_id=1, source_target_pairs={{0,24},{4,28},{8,16},{12,20},{16,8},{20,12},{24,0},{28,4},{1,25},{... | collective-permute-start | bytes 1179656 | tf_op jit(solution)/shard_map/ppermute | solution.py:79
  362.1 27.7 %collective-permute-start.40 = (bf16[256,768]{1,0:T(8,128)(2,1)}, bf16[256,768]{1,0:T(8,128)(2,1)}, u32[]{:S(2)}, u32[]{:S(2)}) collective-permute-start(bf16[256,768]{1,0:T(8,128)(2,1)} %get-tuple-element.114), channel_id=1, source_target_pairs={{0,28},{4,24},{8,20},{12,16},{16,12},{20,8},{24,4},{28,0},{1,29},{... | collective-permute-start | bytes 1179656 | tf_op jit(solution)/shard_map/ppermute | solution.py:79
  (73 other events, 1337.1 us)
where the time goes:
time: 408 us; the launch traced here: 407 us
  Pallas kernels  180 us (44%)
  starting transfers between devices  117 us (29%)
  waiting for transfers between devices  96.9 us (24%)
  other arithmetic  8.07 us (2%)
    pallas_call x4, Pallas kernels, kernel_call(): pl.pallas_call(kernel, out_shape=out_shape, grid_spec=pltpu.PrefetchScala...  154 us
    ppermute x42, waiting for transfers between devices, swap(): return lax.ppermute(value, ('ctx', 'head'), pairs)  92.6 us
    ppermute x42, starting transfers between devices, swap(): return lax.ppermute(value, ('ctx', 'head'), pairs)  86.8 us
    ppermute x12, starting transfers between devices, shift(): return lax.ppermute(value, ('ctx', 'head'), pairs)  30.6 us
    pallas_call x7, Pallas kernels, copy_call(): pl.pallas_call(kernel, out_shape=outs, in_specs=specs, out_specs=[out_spe...  23.2 us
  transfers between devices with their start and end apart: 54, of which 15 were waited for; matrix products, arithmetic and copies ran while one was open for 2% of the time, Pallas kernels for 33%

commit v1 on v0

--- a/solution.py
+++ b/solution.py
@@ -333,11 +333,8 @@
             return c
 
         lax.fori_loop(0, live, scores, 0)
-        stats = jnp.zeros(shape, jnp.float32)
         for g in range(heads):
-            top = spread(jnp.max(m_scr[g], axis=1, keepdims=True), shape)
-            m_scr[g] = top
-            stats = jnp.where(lane == g, top, stats)
+            m_scr[g] = spread(jnp.max(m_scr[g], axis=1, keepdims=True), shape)
         o_acc[...] = jnp.zeros_like(o_acc)
 
         def weigh(i, c):
@@ -352,9 +349,11 @@
             return c
 
         lax.fori_loop(0, live, weigh, 0)
+        stats = jnp.zeros(shape, jnp.float32)
         for g in range(heads):
-            o_scr[x % 2, :, COLS[g]] = o_acc[g, :, :HEAD_WIDTH]
-            stats = jnp.where(lane == heads + g, o_acc[g, :, HEAD_WIDTH:], stats)
+            total = o_acc[g, :, HEAD_WIDTH:]
+            o_scr[x % 2, :, COLS[g]] = o_acc[g, :, :HEAD_WIDTH] * (1.0 / total)
+            stats = jnp.where(lane == g, m_scr[g] + jnp.log(total) / SCORE_SCALE, stats)
         st_scr[x] = stats
         at_place(x, saves, start_all)
         return carry
@@ -378,7 +377,7 @@
     outs, (do_out, stat_out, gq_out) = take(lay.group), take(3)
     to_below, to_above = take(lay.line - 1), take(lay.line - 1)
     q_scr, do_scr, sum_scr, k_tab, v_tab, dk_acc, dv_acc, s_scr, e_scr, m_scr = refs[:10]
-    o_acc, o_scr, st_scr, sems = refs[10:]
+    o_acc, o_scr, st_scr, begun_scr, sems = refs[10:]
     u, w = where_ref[0], where_ref[1]
     heads = GROUP_WIDTH
     made = Copies(sems)
@@ -440,7 +439,9 @@
                 run(jnp.where(block < first, block, block - lay.group))
 
         for g in range(heads):
-            m_scr[g] = spread(st_scr[x, :, g : g + 1], shape)
+            begun = spread(st_scr[x, :, g : g + 1], shape)
+            m_scr[g] = begun
+            begun_scr[g] = begun
 
         def scores(i, c):
             def run(block):
@@ -456,11 +457,9 @@
         stats = jnp.zeros(shape, jnp.float32)
         for g in range(heads):
             top = spread(jnp.max(m_scr[g], axis=1, keepdims=True), shape)
-            old = spread(st_scr[x, :, g : g + 1], shape)
-            total = spread(st_scr[x, :, heads + g : heads + g + 1], shape)
-            fade = jnp.exp2((old - top) * EXP2_SCALE)
+            fade = jnp.exp2((begun_scr[g] - top) * EXP2_SCALE)
             o_acc[g, :, :HEAD_WIDTH] = sum_scr[x, :, COLS[g]] * fade
-            o_acc[g, :, HEAD_WIDTH:] = total * fade
+            o_acc[g, :, HEAD_WIDTH:] = fade
             m_scr[g] = top
             stats = jnp.where(lane == g, top, stats)
 
@@ -709,6 +708,7 @@
         pltpu.VMEM((GROUP_WIDTH, lay.tokens, 2 * HEAD_WIDTH), f32),
         pltpu.VMEM((2, lay.tokens, width), bf),
         pltpu.VMEM(stats, f32),
+        pltpu.VMEM((GROUP_WIDTH, lay.tokens, HEAD_WIDTH), f32),
         pltpu.SemaphoreType.DMA((8 * lay.group + 4 * far,)),
     ]
     table = (2, lay.group, lay.tokens, HEAD_WIDTH)

time: 408 us -> 404 us (level)
  no operation moved by 1% of the time
where the time goes in v1:
time: 404 us; the launch traced here: 403 us
  Pallas kernels  176 us (44%)
  starting transfers between devices  118 us (29%)
  waiting for transfers between devices  96.4 us (24%)
  other arithmetic  8.07 us (2%)
    pallas_call x4, Pallas kernels, kernel_call(): pl.pallas_call(kernel, out_shape=out_shape, grid_spec=pltpu.PrefetchScala...  150 us
    ppermute x42, waiting for transfers between devices, swap(): return lax.ppermute(value, ('ctx', 'head'), pairs)  92.2 us
    ppermute x42, starting transfers between devices, swap(): return lax.ppermute(value, ('ctx', 'head'), pairs)  87.2 us
    ppermute x12, starting transfers between devices, shift(): return lax.ppermute(value, ('ctx', 'head'), pairs)  30.6 us
    pallas_call x7, Pallas kernels, copy_call(): pl.pallas_call(kernel, out_shape=outs, in_specs=specs, out_specs=[out_spe...  23.2 us
  transfers between devices with their start and end apart: 54, of which 15 were waited for; matrix products, arithmetic and copies ran while one was open for 2% of the time, Pallas kernels for 33%

profile of v1, /device:TPU:1, one launch (start us, length us, event | category | flops | bytes accessed | tf_op | source)
XLA Modules:
  0.0 403.0 jit_solution(10463309013815616948)
XLA Ops:
  13.8 6.6 %collective-permute-done.18.refs_5_ = bf16[2,256,128]{2,1,0:T(8,128)(2,1)S(1)} collective-permute-done((bf16[2,256,128]{2,1,0:T(8,128)(2,1)}, bf16[2,256,128]{2,1,0:T(8,128)(2,1)S(1)}, u32[]{:S(2)}, u32[]{:S(2)}) %collective-permute-start.18) | collective-permute-done | bytes 131104 | tf_op jit(solution)/shard_map/ppermute | solution.py:79
  24.8 5.0 %collective-permute-start.21 = (bf16[2,8,256,128]{3,2,1,0:T(8,128)(2,1)}, bf16[2,8,256,128]{3,2,1,0:T(8,128)(2,1)}, u32[]{:S(2)}, u32[]{:S(2)}) collective-permute-start(bf16[2,8,256,128]{3,2,1,0:T(8,128)(2,1)} %shard_map.96.refs_8_.refs_7_), channel_id=1, source_target_pairs={{0,1},{4,5},{8,9},{12,13},{16,17},{20,21},{24,25},{28,29},{1,2},{5... | collective-permute-start | bytes 3145736 | tf_op jit(solution)/shard_map/ppermute | solution.py:85
  29.9 3.5 shard_map.94
  40.8 4.0 %collective-permute-done.8.refs_10_ = bf16[256,768]{1,0:T(8,128)(2,1)S(1)} collective-permute-done((bf16[256,768]{1,0:T(8,128)(2,1)}, bf16[256,768]{1,0:T(8,128)(2,1)S(1)}, u32[]{:S(2)}, u32[]{:S(2)}) %collective-permute-start.8) | collective-permute-done | bytes 393248 | tf_op jit(solution)/shard_map/ppermute | solution.py:79
  46.3 4.2 %collective-permute-done.22.refs_10_.refs_21_.refs_9_ = bf16[2,8,256,128]{3,2,1,0:T(8,128)(2,1)S(1)} collective-permute-done((bf16[2,8,256,128]{3,2,1,0:T(8,128)(2,1)}, bf16[2,8,256,128]{3,2,1,0:T(8,128)(2,1)S(1)}, u32[]{:S(2)}, u32[]{:S(2)}) %collective-permute-start.22) | collective-permute-done | bytes 1048608 | tf_op jit(solution)/shard_map/ppermute | solution.py:85
  57.4 6.6 %collective-permute-done.1.refs_2_.refs_3_ = bf16[256,768]{1,0:T(8,128)(2,1)S(1)} collective-permute-done((bf16[256,768]{1,0:T(8,128)(2,1)}, bf16[256,768]{1,0:T(8,128)(2,1)S(1)}, u32[]{:S(2)}, u32[]{:S(2)}) %collective-permute-start.1) | collective-permute-done | bytes 393248 | tf_op jit(solution)/shard_map/ppermute | solution.py:79
  63.9 3.8 collective-permute-start.4
  67.7 5.7 %collective-permute-done.2.refs_3_.refs_4_ = bf16[256,768]{1,0:T(8,128)(2,1)S(1)} collective-permute-done((bf16[256,768]{1,0:T(8,128)(2,1)}, bf16[256,768]{1,0:T(8,128)(2,1)S(1)}, u32[]{:S(2)}, u32[]{:S(2)}) %collective-permute-start.2) | collective-permute-done | bytes 393248 | tf_op jit(solution)/shard_map/ppermute | solution.py:79
  79.1 7.4 %collective-permute-done.5.refs_6_.refs_7_.refs_2_ = bf16[256,768]{1,0:T(8,128)(2,1)S(1)} collective-permute-done((bf16[256,768]{1,0:T(8,128)(2,1)}, bf16[256,768]{1,0:T(8,128)(2,1)S(1)}, u32[]{:S(2)}, u32[]{:S(2)}) %collective-permute-start.5) | collective-permute-done | bytes 393248 | tf_op jit(solution)/shard_map/ppermute | solution.py:79
  88.7 6.2 %collective-permute-done.6.refs_7_.refs_8_.refs_3_ = bf16[256,768]{1,0:T(8,128)(2,1)S(1)} collective-permute-done((bf16[256,768]{1,0:T(8,128)(2,1)}, bf16[256,768]{1,0:T(8,128)(2,1)S(1)}, u32[]{:S(2)}, u32[]{:S(2)}) %collective-permute-start.6) | collective-permute-done | bytes 393248 | tf_op jit(solution)/shard_map/ppermute | solution.py:79
  100.7 36.1 %shard_map.97 = (f32[8,256,768]{2,1,0:T(8,128)}, f32[8,256,128]{2,1,0:T(8,128)}) custom-call(s32[16,8]{1,0:T(8,128)} %copy.13.list_ref, s32[16]{0:T(128)} %count_ref.7, s32[2]{0:T(128)} %pad_add_fusion.refs_0_.where_ref, bf16[256,6144]{1,0:T(8,128)(2,1)} %refs_0_.5, bf16[256,768]{1,0:T(8,128)(2,1)} %copy-done.27, bf16[256,768]{1,0:T(8,128)(2,1)} %copy-done.33, ...), custom_call_target="tpu_custom_call" | custom-call | flops 19327352832 | bytes 16777216 | tf_op jit(solution)/shard_map/pallas_call | solution.py:645
  136.8 33.8 %shard_map.98 = (bf16[256,768]{1,0:T(8,128)(2,1)}, bf16[256,768]{1,0:T(8,128)(2,1)}, bf16[256,768]{1,0:T(8,128)(2,1)}, bf16[256,768]{1,0:T(8,128)(2,1)}, bf16[25...) custom-call(s32[16,8]{1,0:T(8,128)} %copy.13.list_ref, ...), custom_call_target="tpu_custom_call" | custom-call | flops 38654705664 | bytes 16777216 | tf_op jit(solution)/shard_map/pallas_call | solution.py:645
  172.8 10.0 %collective-permute-start.41 = (bf16[2,8,256,128]{3,2,1,0:T(8,128)(2,1)}, bf16[2,8,256,128]{3,2,1,0:T(8,128)(2,1)}, u32[]{:S(2)}, u32[]{:S(2)}) collective-permute-start(bf16[2,8,256,128]{3,2,1,0:T(8,128)(2,1)} %get-tuple-element.116), channel_id=1, source_target_pairs={{0,1},{4,5},{8,9},{12,13},{16,17},{20,21},{24,25},{28,29}} | collective-permute-start | bytes 3145736 | tf_op jit(solution)/shard_map/ppermute | solution.py:85
  184.5 45.3 %shard_map.100 = (bf16[256,768]{1,0:T(8,128)(2,1)}, bf16[256,768]{1,0:T(8,128)(2,1)}, bf16[256,768]{1,0:T(8,128)(2,1)}, bf16[256,768]{1,0:T(8,128)(2,1)}, f32[8,...) custom-call(s32[16,8]{1,0:T(8,128)} %copy.13.list_ref, s32[16]{0:T(128)} %count_ref.7, s32[2]{0:T(128)} %pad_add_fusion.refs_0_.where_ref, ...), custom_call_target="tpu_custom_call" | custom-call | flops 19327352832 | bytes 16777216 | tf_op jit(solution)/shard_map/pallas_call | solution.py:645
  237.9 34.4 %shard_map.101 = (bf16[256,768]{1,0:T(8,128)(2,1)}, bf16[256,768]{1,0:T(8,128)(2,1)}, bf16[256,768]{1,0:T(8,128)(2,1)}, bf16[256,768]{1,0:T(8,128)(2,1)}, bf16[2...) custom-call(s32[16,8]{1,0:T(8,128)} %copy.13.list_ref, ...), custom_call_target="tpu_custom_call", output_to_operand_aliasing={{5}: (15, {}), {6}: (16, {})} | custom-call | flops 19327352832 | bytes 16777216 | tf_op jit(solution)/shard_map/pallas_call | solution.py:645
  278.7 29.9 %collective-permute-start.30 = (bf16[256,768]{1,0:T(8,128)(2,1)S(1)}, bf16[256,768]{1,0:T(8,128)(2,1)S(1)}, u32[]{:S(2)}, u32[]{:S(2)}) collective-permute-start(bf16[256,768]{1,0:T(8,128)(2,1)S(1)} %copy-done.40), channel_id=1, source_target_pairs={{0,16},{4,20},{8,24},{12,28},{16,0},{20,4},{24,8},{28,12},{1,17},{... | collective-permute-start | bytes 1179656 | tf_op jit(solution)/shard_map/ppermute | solution.py:79
  311.7 14.3 %collective-permute-done.30.refs_5_ = bf16[256,768]{1,0:T(8,128)(2,1)S(1)} collective-permute-done((bf16[256,768]{1,0:T(8,128)(2,1)S(1)}, bf16[256,768]{1,0:T(8,128)(2,1)S(1)}, u32[]{:S(2)}, u32[]{:S(2)}) %collective-permute-start.30) | collective-permute-done | bytes 393248 | tf_op jit(solution)/shard_map/ppermute | solution.py:79
  326.0 4.3 %collective-permute-start.33 = (bf16[256,768]{1,0:T(8,128)(2,1)S(1)}, bf16[256,768]{1,0:T(8,128)(2,1)S(1)}, u32[]{:S(2)}, u32[]{:S(2)}) collective-permute-start(bf16[256,768]{1,0:T(8,128)(2,1)S(1)} %copy-done.34), channel_id=1, source_target_pairs={{0,28},{4,24},{8,20},{12,16},{16,12},{20,8},{24,4},{28,0},{1,29},{... | collective-permute-start | bytes 1179656 | tf_op jit(solution)/shard_map/ppermute | solution.py:79
  330.3 13.0 %collective-permute-done.31.refs_6_ = bf16[256,768]{1,0:T(8,128)(2,1)S(1)} collective-permute-done((bf16[256,768]{1,0:T(8,128)(2,1)S(1)}, bf16[256,768]{1,0:T(8,128)(2,1)S(1)}, u32[]{:S(2)}, u32[]{:S(2)}) %collective-permute-start.31) | collective-permute-done | bytes 393248 | tf_op jit(solution)/shard_map/ppermute | solution.py:79
  346.9 6.7 %collective-permute-done.35.refs_3_ = bf16[256,768]{1,0:T(8,128)(2,1)S(1)} collective-permute-done((bf16[256,768]{1,0:T(8,128)(2,1)S(1)}, bf16[256,768]{1,0:T(8,128)(2,1)S(1)}, u32[]{:S(2)}, u32[]{:S(2)}) %collective-permute-start.35) | collective-permute-done | bytes 393248 | tf_op jit(solution)/shard_map/ppermute | solution.py:79
  353.7 3.5 collective-permute-start.38
  365.2 18.5 %collective-permute-done.38.refs_6_ = bf16[256,768]{1,0:T(8,128)(2,1)} collective-permute-done((bf16[256,768]{1,0:T(8,128)(2,1)}, bf16[256,768]{1,0:T(8,128)(2,1)}, u32[]{:S(2)}, u32[]{:S(2)}) %collective-permute-start.38) | collective-permute-done | bytes 393248 | tf_op jit(solution)/shard_map/ppermute | solution.py:79
  389.7 4.3 %shard_map.99 = bf16[256,6144]{1,0:T(8,128)(2,1)} custom-call(s32[2]{0:T(128)} %pad_add_fusion.refs_0_.where_ref, bf16[256,768]{1,0:T(8,128)(2,1)} %get-tuple-element.92.refs_1_, bf16[256,768]{1,0:T(8,128)(2,1)} %copy-done.5, bf16[256,768]{1,0:T(8,128)(2,1)} %copy-done.6, bf16[256,768]{1,0:T(8,128)(2,1)} %collective-permute-done.29.refs_4_, ...), custom_call_target="tpu_custom_call" | custom-call | bytes 6291456 | tf_op jit(solution)/shard_map/pallas_call | solution.py:108
  394.0 4.3 %shard_map.102 = bf16[256,6144]{1,0:T(8,128)(2,1)} custom-call(s32[2]{0:T(128)} %pad_add_fusion.refs_0_.where_ref, bf16[256,768]{1,0:T(8,128)(2,1)} %get-tuple-element.103.refs_1_, bf16[256,768]{1,0:T(8,128)(2,1)} %copy-done.11, bf16[256,768]{1,0:T(8,128)(2,1)} %copy-done.12, bf16[256,768]{1,0:T(8,128)(2,1)} %collective-permute-done.36.refs_4_, ...), custom_call_target="tpu_custom_call" | custom-call | bytes 6291456 | tf_op jit(solution)/shard_map/pallas_call | solution.py:108
  (188 shorter events, 90.0 us)
Async XLA Ops:
  23.5 27.0 %collective-permute-start.22 = (bf16[2,8,256,128]{3,2,1,0:T(8,128)(2,1)}, bf16[2,8,256,128]{3,2,1,0:T(8,128)(2,1)S(1)}, u32[]{:S(2)}, u32[]{:S(2)}) collective-permute-start(bf16[2,8,256,128]{3,2,1,0:T(8,128)(2,1)} %shard_map.96.refs_8_.refs_7_), channel_id=1, source_target_pairs={{1,0},{5,4},{9,8},{13,12},{17,16},{21,20},{25,24},{29,28},{2,1},{6... | collective-permute-start | bytes 3145736 | tf_op jit(solution)/shard_map/ppermute | solution.py:85
  24.8 27.0 %collective-permute-start.21 = (bf16[2,8,256,128]{3,2,1,0:T(8,128)(2,1)}, bf16[2,8,256,128]{3,2,1,0:T(8,128)(2,1)}, u32[]{:S(2)}, u32[]{:S(2)}) collective-permute-start(bf16[2,8,256,128]{3,2,1,0:T(8,128)(2,1)} %shard_map.96.refs_8_.refs_7_), channel_id=1, source_target_pairs={{0,1},{4,5},{8,9},{12,13},{16,17},{20,21},{24,25},{28,29},{1,2},{5... | collective-permute-start | bytes 3145736 | tf_op jit(solution)/shard_map/ppermute | solution.py:85
  50.5 47.2 %collective-permute-start.25 = (bf16[2,8,256,128]{3,2,1,0:T(8,128)(2,1)S(1)}, bf16[2,8,256,128]{3,2,1,0:T(8,128)(2,1)}, u32[]{:S(2)}, u32[]{:S(2)}) collective-permute-start(bf16[2,8,256,128]{3,2,1,0:T(8,128)(2,1)S(1)} %collective-permute-done.22.refs_10_.refs_21_.refs_9_), channel_id=1, source_target_pairs={{1,0},{5,4},{9,8},{13,12},{17,16},{21,20},{25,24},{29,28},{2,1},{6... | collective-permute-start | bytes 3145736 | tf_op jit(solution)/shard_map/ppermute | solution.py:85
  51.8 47.2 %collective-permute-start.23 = (bf16[2,8,256,128]{3,2,1,0:T(8,128)(2,1)}, bf16[2,8,256,128]{3,2,1,0:T(8,128)(2,1)}, u32[]{:S(2)}, u32[]{:S(2)}) collective-permute-start(bf16[2,8,256,128]{3,2,1,0:T(8,128)(2,1)} %collective-permute-done.21.refs_9_.refs_18_.refs_8_), channel_id=1, source_target_pairs={{1,2},{5,6},{9,10},{13,14},{17,18},{21,22},{25,26},{29,30},{2,3},{... | collective-permute-start | bytes 3145736 | tf_op jit(solution)/shard_map/ppermute | solution.py:85
  77.7 59.0 %collective-permute-start.11 = (bf16[256,768]{1,0:T(8,128)(2,1)}, bf16[256,768]{1,0:T(8,128)(2,1)}, u32[]{:S(2)}, u32[]{:S(2)}) collective-permute-start(bf16[256,768]{1,0:T(8,128)(2,1)} %get-tuple-element.79), channel_id=1, source_target_pairs={{0,20},{4,16},{8,28},{12,24},{16,4},{20,0},{24,12},{28,8},{1,21},{... | collective-permute-start | bytes 1179656 | tf_op jit(solution)/shard_map/ppermute | solution.py:79
  86.5 50.3 %collective-permute-start.12 = (bf16[256,768]{1,0:T(8,128)(2,1)}, bf16[256,768]{1,0:T(8,128)(2,1)}, u32[]{:S(2)}, u32[]{:S(2)}) collective-permute-start(bf16[256,768]{1,0:T(8,128)(2,1)} %get-tuple-element.80), channel_id=1, source_target_pairs={{0,24},{4,28},{8,16},{12,20},{16,8},{20,12},{24,0},{28,4},{1,25},{... | collective-permute-start | bytes 1179656 | tf_op jit(solution)/shard_map/ppermute | solution.py:79
  94.9 41.8 %collective-permute-start.13 = (bf16[256,768]{1,0:T(8,128)(2,1)}, bf16[256,768]{1,0:T(8,128)(2,1)}, u32[]{:S(2)}, u32[]{:S(2)}) collective-permute-start(bf16[256,768]{1,0:T(8,128)(2,1)} %get-tuple-element.81), channel_id=1, source_target_pairs={{0,28},{4,24},{8,20},{12,16},{16,12},{20,8},{24,4},{28,0},{1,29},{... | collective-permute-start | bytes 1179656 | tf_op jit(solution)/shard_map/ppermute | solution.py:79
  97.7 39.1 %collective-permute-start.26 = (bf16[2,8,256,128]{3,2,1,0:T(8,128)(2,1)}, bf16[2,8,256,128]{3,2,1,0:T(8,128)(2,1)}, u32[]{:S(2)}, u32[]{:S(2)}) collective-permute-start(bf16[2,8,256,128]{3,2,1,0:T(8,128)(2,1)} %collective-permute-done.25.refs_22_), channel_id=1, source_target_pairs={{1,0},{5,4},{9,8},{13,12},{17,16},{21,20},{25,24},{29,28}} | collective-permute-start | bytes 3145736 | tf_op jit(solution)/shard_map/ppermute | solution.py:85
  99.0 37.8 %collective-permute-start.24 = (bf16[2,8,256,128]{3,2,1,0:T(8,128)(2,1)}, bf16[2,8,256,128]{3,2,1,0:T(8,128)(2,1)}, u32[]{:S(2)}, u32[]{:S(2)}) collective-permute-start(bf16[2,8,256,128]{3,2,1,0:T(8,128)(2,1)} %collective-permute-done.23.refs_19_), channel_id=1, source_target_pairs={{2,3},{6,7},{10,11},{14,15},{18,19},{22,23},{26,27},{30,31}} | collective-permute-start | bytes 3145736 | tf_op jit(solution)/shard_map/ppermute | solution.py:85
  170.6 108.0 %collective-permute-start.27 = (bf16[256,768]{1,0:T(8,128)(2,1)}, bf16[256,768]{1,0:T(8,128)(2,1)S(1)}, u32[]{:S(2)}, u32[]{:S(2)}) collective-permute-start(bf16[256,768]{1,0:T(8,128)(2,1)} %get-tuple-element.93), channel_id=1, source_target_pairs={{0,4},{4,0},{8,12},{12,8},{16,20},{20,16},{24,28},{28,24},{1,5},{5... | collective-permute-start | bytes 1179656 | tf_op jit(solution)/shard_map/ppermute | solution.py:79
  170.7 137.9 %collective-permute-start.28 = (bf16[256,768]{1,0:T(8,128)(2,1)}, bf16[256,768]{1,0:T(8,128)(2,1)S(1)}, u32[]{:S(2)}, u32[]{:S(2)}) collective-permute-start(bf16[256,768]{1,0:T(8,128)(2,1)} %get-tuple-element.94), channel_id=1, source_target_pairs={{0,8},{4,12},{8,0},{12,4},{16,24},{20,28},{24,16},{28,20},{1,9},{5... | collective-permute-start | bytes 1179656 | tf_op jit(solution)/shard_map/ppermute | solution.py:79
  171.0 138.1 %collective-permute-start.29 = (bf16[256,768]{1,0:T(8,128)(2,1)}, bf16[256,768]{1,0:T(8,128)(2,1)}, u32[]{:S(2)}, u32[]{:S(2)}) collective-permute-start(bf16[256,768]{1,0:T(8,128)(2,1)} %get-tuple-element.95), channel_id=1, source_target_pairs={{0,12},{4,8},{8,4},{12,0},{16,28},{20,24},{24,20},{28,16},{1,13},{... | collective-permute-start | bytes 1179656 | tf_op jit(solution)/shard_map/ppermute | solution.py:79
  172.8 57.0 %collective-permute-start.41 = (bf16[2,8,256,128]{3,2,1,0:T(8,128)(2,1)}, bf16[2,8,256,128]{3,2,1,0:T(8,128)(2,1)}, u32[]{:S(2)}, u32[]{:S(2)}) collective-permute-start(bf16[2,8,256,128]{3,2,1,0:T(8,128)(2,1)} %get-tuple-element.116), channel_id=1, source_target_pairs={{0,1},{4,5},{8,9},{12,13},{16,17},{20,21},{24,25},{28,29}} | collective-permute-start | bytes 3145736 | tf_op jit(solution)/shard_map/ppermute | solution.py:85
  182.8 51.9 %collective-permute-start.44 = (bf16[2,8,256,128]{3,2,1,0:T(8,128)(2,1)}, bf16[2,8,256,128]{3,2,1,0:T(8,128)(2,1)}, u32[]{:S(2)}, u32[]{:S(2)}) collective-permute-start(bf16[2,8,256,128]{3,2,1,0:T(8,128)(2,1)} %get-tuple-element.119), channel_id=1, source_target_pairs={{3,2},{7,6},{11,10},{15,14},{19,18},{23,22},{27,26},{31,30}} | collective-permute-start | bytes 3145736 | tf_op jit(solution)/shard_map/ppermute | solution.py:85
  232.4 39.9 %collective-permute-start.42 = (bf16[2,8,256,128]{3,2,1,0:T(8,128)(2,1)}, bf16[2,8,256,128]{3,2,1,0:T(8,128)(2,1)}, u32[]{:S(2)}, u32[]{:S(2)}) collective-permute-start(bf16[2,8,256,128]{3,2,1,0:T(8,128)(2,1)} %add_convert_fusion.3), channel_id=1, source_target_pairs={{0,1},{4,5},{8,9},{12,13},{16,17},{20,21},{24,25},{28,29},{1,2},{5... | collective-permute-start | bytes 3145736 | tf_op jit(solution)/shard_map/ppermute | solution.py:85
  236.3 39.6 %collective-permute-start.45 = (bf16[2,8,256,128]{3,2,1,0:T(8,128)(2,1)S(1)}, bf16[2,8,256,128]{3,2,1,0:T(8,128)(2,1)}, u32[]{:S(2)}, u32[]{:S(2)}) collective-permute-start(bf16[2,8,256,128]{3,2,1,0:T(8,128)(2,1)S(1)} %add_convert_fusion.1), channel_id=1, source_target_pairs={{2,1},{6,5},{10,9},{14,13},{18,17},{22,21},{26,25},{30,29},{3,2},{... | collective-permute-start | bytes 3145736 | tf_op jit(solution)/shard_map/ppermute | solution.py:85
  274.3 82.8 %collective-permute-start.43 = (bf16[2,8,256,128]{3,2,1,0:T(8,128)(2,1)S(1)}, bf16[2,8,256,128]{3,2,1,0:T(8,128)(2,1)S(1)}, u32[]{:S(2)}, u32[]{:S(2)}) collective-permute-start(bf16[2,8,256,128]{3,2,1,0:T(8,128)(2,1)S(1)} %add_convert_fusion.2), channel_id=1, source_target_pairs={{0,1},{4,5},{8,9},{12,13},{16,17},{20,21},{24,25},{28,29},{1,2},{5... | collective-permute-start | bytes 3145736 | tf_op jit(solution)/shard_map/ppermute | solution.py:85
  277.4 80.8 %collective-permute-start.46 = (bf16[2,8,256,128]{3,2,1,0:T(8,128)(2,1)S(1)}, bf16[2,8,256,128]{3,2,1,0:T(8,128)(2,1)S(1)}, u32[]{:S(2)}, u32[]{:S(2)}) collective-permute-start(bf16[2,8,256,128]{3,2,1,0:T(8,128)(2,1)S(1)} %add_convert_fusion), channel_id=1, source_target_pairs={{1,0},{5,4},{9,8},{13,12},{17,16},{21,20},{25,24},{29,28},{2,1},{6... | collective-permute-start | bytes 3145736 | tf_op jit(solution)/shard_map/ppermute | solution.py:85
  278.7 47.3 %collective-permute-start.30 = (bf16[256,768]{1,0:T(8,128)(2,1)S(1)}, bf16[256,768]{1,0:T(8,128)(2,1)S(1)}, u32[]{:S(2)}, u32[]{:S(2)}) collective-permute-start(bf16[256,768]{1,0:T(8,128)(2,1)S(1)} %copy-done.40), channel_id=1, source_target_pairs={{0,16},{4,20},{8,24},{12,28},{16,0},{20,4},{24,8},{28,12},{1,17},{... | collective-permute-start | bytes 1179656 | tf_op jit(solution)/shard_map/ppermute | solution.py:79
  308.6 34.7 %collective-permute-start.31 = (bf16[256,768]{1,0:T(8,128)(2,1)S(1)}, bf16[256,768]{1,0:T(8,128)(2,1)S(1)}, u32[]{:S(2)}, u32[]{:S(2)}) collective-permute-start(bf16[256,768]{1,0:T(8,128)(2,1)S(1)} %copy-done.39), channel_id=1, source_target_pairs={{0,20},{4,16},{8,28},{12,24},{16,4},{20,0},{24,12},{28,8},{1,21},{... | collective-permute-start | bytes 1179656 | tf_op jit(solution)/shard_map/ppermute | solution.py:79
  309.1 34.2 %collective-permute-start.32 = (bf16[256,768]{1,0:T(8,128)(2,1)S(1)}, bf16[256,768]{1,0:T(8,128)(2,1)S(1)}, u32[]{:S(2)}, u32[]{:S(2)}) collective-permute-start(bf16[256,768]{1,0:T(8,128)(2,1)S(1)} %copy-done.38), channel_id=1, source_target_pairs={{0,24},{4,28},{8,16},{12,20},{16,8},{20,12},{24,0},{28,4},{1,25},{... | collective-permute-start | bytes 1179656 | tf_op jit(solution)/shard_map/ppermute | solution.py:79
  353.7 30.1 %collective-permute-start.38 = (bf16[256,768]{1,0:T(8,128)(2,1)}, bf16[256,768]{1,0:T(8,128)(2,1)}, u32[]{:S(2)}, u32[]{:S(2)}) collective-permute-start(bf16[256,768]{1,0:T(8,128)(2,1)} %get-tuple-element.112), channel_id=1, source_target_pairs={{0,20},{4,16},{8,28},{12,24},{16,4},{20,0},{24,12},{28,8},{1,21},{... | collective-permute-start | bytes 1179656 | tf_op jit(solution)/shard_map/ppermute | solution.py:79
  357.2 28.1 %collective-permute-start.39 = (bf16[256,768]{1,0:T(8,128)(2,1)}, bf16[256,768]{1,0:T(8,128)(2,1)}, u32[]{:S(2)}, u32[]{:S(2)}) collective-permute-start(bf16[256,768]{1,0:T(8,128)(2,1)} %get-tuple-element.113), channel_id=1, source_target_pairs={{0,24},{4,28},{8,16},{12,20},{16,8},{20,12},{24,0},{28,4},{1,25},{... | collective-permute-start | bytes 1179656 | tf_op jit(solution)/shard_map/ppermute | solution.py:79
  358.2 27.7 %collective-permute-start.40 = (bf16[256,768]{1,0:T(8,128)(2,1)}, bf16[256,768]{1,0:T(8,128)(2,1)}, u32[]{:S(2)}, u32[]{:S(2)}) collective-permute-start(bf16[256,768]{1,0:T(8,128)(2,1)} %get-tuple-element.114), channel_id=1, source_target_pairs={{0,28},{4,24},{8,20},{12,16},{16,12},{20,8},{24,4},{28,0},{1,29},{... | collective-permute-start | bytes 1179656 | tf_op jit(solution)/shard_map/ppermute | solution.py:79
  (73 other events, 1337.4 us)
